TPU v7x, 256 devices: a whole 4x4x8 slice. The times are simulated.
256 devices in a mesh: tile: 128 (over y, z, x), sub: 2 (over core).
Axes of the slice: x: 4, y: 4, z: 8, core: 2. Of those that a mesh axis runs over, the one named last changes fastest.
Arguments:
- right_side: float32 [2, 32768, 256], P(None, ('tile', 'sub')), may hold values from -12 to 12
- pixel_weight: float32 [32768, 256], P(('tile', 'sub')), may hold values from 0.5 to 2
- noise_diag: float32 [2, 32768, 256], P(None, ('tile', 'sub')), may hold values from 0.5 to 8
- noise_corr: float32 [32768, 256], P(('tile', 'sub')), may hold values from -0.8 to 0.8
- neighbours: int32 [3, 4, 128], replicated, may hold values from 0 to 127, as said below
Outputs:
- solution: float32 [2, 32768, 256], P(None, ('tile', 'sub'))
- final_misfit: float32 [2, 32768, 256], P(None, ('tile', 'sub'))
Inputs may be any that keep to these rules, and one draw needn't show every extreme that they name: `neighbours`: across side 0 lies side 1 of another or the same tile and across side 2 lies side 3, and conversely; the relation is symmetric, with the same reversal flag on both sides of an edge. Every neighbour lies, in the cyclic order of tiles, within 3 places of its tile or within 3 places of the tile 128/2 places away, and 3 places is reached. Flags are 0 or 1.
All inputs are finite; a program needn't handle non-finite values.
Results may differ from a plain program's by a relative error of at most 0.00012.
Values sent between devices are 32-bit elements; how exact they have to be, the bound alone decides.
A program may use at most 128 MiB of HBM per device.

v0:
```python
import jax
import jax.numpy as jnp
from jax import lax
from jax.sharding import PartitionSpec as P

NU = 2
NC = 3
MASS = 0.05
OMEGA = 0.8


def with_halo(block, sides, width):
    for axis, dim in sides:
        count = lax.axis_size(axis)
        forward = [(i, i + 1) for i in range(count - 1)]
        backward = [(target, source) for source, target in forward]
        low = lax.ppermute(
            lax.slice_in_dim(block, block.shape[dim] - width, None, axis=dim), axis, forward
        )
        high = lax.ppermute(lax.slice_in_dim(block, 0, width, axis=dim), axis, backward)
        block = jnp.concatenate([low, block, high], axis=dim)
    return block


def inverse_blocks(diag_term, noise_terms):
    upper_left = diag_term + noise_terms[0]
    lower_right = diag_term + noise_terms[1]
    determinant = upper_left * lower_right - noise_terms[2] * noise_terms[2]
    return jnp.stack(
        [lower_right / determinant, upper_left / determinant, -noise_terms[2] / determinant]
    )


def apply_block(inverse, misfit):
    out_first = inverse[0] * misfit[0] + inverse[2] * misfit[1]
    second = inverse[2] * misfit[0] + inverse[1] * misfit[1]
    return jnp.stack([out_first, second])


def coarsen_sum(values):
    old_shape = values.shape
    new_shape = old_shape[:-2] + (old_shape[-2] // 2, 2, old_shape[-1] // 2, 2)
    return values.reshape(new_shape).sum(axis=(-3, -1))


def prolong(values):
    return jnp.repeat(jnp.repeat(values, 2, axis=-2), 2, axis=-1)


def across_sides(side_rows, link_cols, grid_level):
    if grid_level == "fine":
        everyone = lax.all_gather(side_rows[None], "tile", axis=0, tiled=True)
    else:
        everyone = lax.all_gather(side_rows[None], "tile", axis=0, tiled=True)
    across = everyone[link_cols[0], link_cols[1]]
    flipped = jnp.flip(across, axis=2)
    return jnp.where(link_cols[2][:, None, None] == 1, flipped, across)


def band_sum(scaled, link_cols, grid_level):
    sub_id = lax.axis_index("sub")
    sub_count = lax.axis_size("sub")
    band_rows = scaled.shape[1]
    band_width = scaled.shape[2]
    if grid_level == "fine":
        padded = with_halo(scaled, (("sub", 1),), 1)
    else:
        padded = with_halo(scaled, (("sub", 1),), 1)
    zeros_row = jnp.zeros((2, band_width), jnp.float32)
    start_row = (jnp.int32(0), sub_id * band_rows)
    top_part = jnp.where(sub_id == 0, scaled[:, 0, :], zeros_row)
    bottom_part = jnp.where(sub_id == sub_count - 1, scaled[:, band_rows - 1, :], zeros_row)
    left_part = lax.dynamic_update_slice(zeros_row, scaled[:, :, 0], start_row)
    right_part = lax.dynamic_update_slice(zeros_row, scaled[:, :, band_width - 1], start_row)
    partial_sides = jnp.stack([top_part, bottom_part, left_part, right_part])
    if grid_level == "fine":
        side_rows = lax.psum(partial_sides, "sub")
    else:
        side_rows = lax.psum(partial_sides, "sub")
    across = across_sides(side_rows, link_cols, grid_level)
    upper_row = padded[:, 0, :] + jnp.where(sub_id == 0, across[0], zeros_row)
    lower_row = padded[:, band_rows + 1, :] + jnp.where(
        sub_id == sub_count - 1, across[1], zeros_row
    )
    left_col = lax.dynamic_slice(across[2], start_row, (2, band_rows))
    right_col = lax.dynamic_slice(across[3], start_row, (2, band_rows))
    above_rows = jnp.concatenate([upper_row[:, None, :], scaled[:, :-1, :]], axis=1)
    below_rows = jnp.concatenate([scaled[:, 1:, :], lower_row[:, None, :]], axis=1)
    west_cols = jnp.concatenate([left_col[:, :, None], scaled[:, :, :-1]], axis=2)
    east_cols = jnp.concatenate([scaled[:, :, 1:], right_col[:, :, None]], axis=2)
    return above_rows + below_rows + west_cols + east_cols


def operate(iterate, weight, stiffness, noise_terms, link_cols, grid_level):
    scaled = weight * iterate
    beside_all = band_sum(scaled, link_cols, grid_level)
    stencil = (MASS + 4.0) * scaled - beside_all
    out_first = (
        stiffness * weight * stencil[0] + noise_terms[0] * iterate[0] + noise_terms[2] * iterate[1]
    )
    second = (
        stiffness * weight * stencil[1] + noise_terms[2] * iterate[0] + noise_terms[1] * iterate[1]
    )
    return jnp.stack([out_first, second])


def relax(iterate, source, weight, stiffness, noise_terms, inverse, link_cols, grid_level):
    misfit = source - operate(iterate, weight, stiffness, noise_terms, link_cols, grid_level)
    return iterate + OMEGA * apply_block(inverse, misfit)


def coarse_solve(coarse_source, coarse_weight, coarse_noise, link_cols):
    coarse_inverse = inverse_blocks(
        2.0 * (MASS + 4.0) * coarse_weight * coarse_weight, coarse_noise
    )
    correction = OMEGA * apply_block(coarse_inverse, coarse_source)
    for sweep_no in range(NC - 1):
        correction = relax(
            correction,
            coarse_source,
            coarse_weight,
            2.0,
            coarse_noise,
            coarse_inverse,
            link_cols,
            "coarse",
        )
    return correction


def body(right_side, pixel_weight, noise_diag, noise_corr, neighbours):
    link_cols = lax.dynamic_slice_in_dim(neighbours, lax.axis_index("tile"), 1, 2)[:, :, 0]
    cross_noise = noise_corr * jnp.sqrt(noise_diag[0] * noise_diag[1])
    noise_terms = jnp.stack([noise_diag[0], noise_diag[1], cross_noise])
    inverse = inverse_blocks((MASS + 4.0) * pixel_weight * pixel_weight, noise_terms)
    iterate = OMEGA * apply_block(inverse, right_side)
    iterate = relax(iterate, right_side, pixel_weight, 1.0, noise_terms, inverse, link_cols, "fine")
    misfit = right_side - operate(iterate, pixel_weight, 1.0, noise_terms, link_cols, "fine")
    coarse_source = coarsen_sum(misfit)
    coarse_weight = 0.25 * coarsen_sum(pixel_weight)
    coarse_noise = coarsen_sum(noise_terms)
    correction = coarse_solve(coarse_source, coarse_weight, coarse_noise, link_cols)
    iterate = iterate + prolong(correction)
    for sweep_no in range(NU):
        iterate = relax(
            iterate, right_side, pixel_weight, 1.0, noise_terms, inverse, link_cols, "fine"
        )
    final_misfit = right_side - operate(iterate, pixel_weight, 1.0, noise_terms, link_cols, "fine")
    return (iterate, final_misfit)


def solution(mesh):
    placed = (
        P(None, ("tile", "sub"), None),
        P(("tile", "sub"), None),
        P(None, ("tile", "sub"), None),
        P(("tile", "sub"), None),
        P(),
    )
    return jax.shard_map(
        body,
        mesh=mesh,
        in_specs=placed,
        out_specs=(P(None, ("tile", "sub"), None), P(None, ("tile", "sub"), None)),
        check_vma=False,
    )
```

profile of v0, /device:TPU:2, one launch (start us, length us, event | category | flops | bytes accessed | tf_op | source)
XLA Modules:
  0.0 1307.8 jit_solution(11690635591361222974)
XLA Ops:
  15.5 3.1 psum.49
  20.0 3.7 collective-permute-start
  28.3 96.1 %all-gather.6.cloned.1.call-done = f32[128,4,2,256]{3,1,2,0:T(4,128)} async-done(((f32[1,4,2,256]{3,1,2,0:T(4,128)}), f32[128,4,2,256]{3,1,2,0:T(4,128)}) %all-gather.6.cloned.1.call-update) | async-done | bytes 1048592 | tf_op jit(solution)/shard_map/all_gather | solution.py:52
  124.4 2.8 copy.1535
  134.6 3.1 psum.50
  137.8 9.8 stack.205
  147.6 18.0 %stack.204 = f32[2,64,2,128,2]{4,3,2,1,0:T(8,128)} reshape(f32[2,128,256]{2,1,0:T(8,128)S(1)} %copy-done.1) | data formatting | bytes 524288 | tf_op jit(solution)/shard_map/stack | solution.py:134
  165.6 9.7 reshape.563
  175.3 4.5 reduce_sum.27
  180.5 12.0 maximum_reduce_fusion
  197.7 41.9 %all-gather.8.cloned.1.call-done = f32[128,4,2,256]{3,1,2,0:T(4,128)} async-done(((f32[1,4,2,256]{3,1,2,0:T(4,128)}), f32[128,4,2,256]{3,1,2,0:T(4,128)}) %all-gather.8.cloned.1.call-update) | async-done | bytes 1048592 | tf_op jit(solution)/shard_map/all_gather | solution.py:52
  244.0 18.1 %reshape.564 = f32[2,64,2,128,2]{4,3,2,1,0:T(8,128)} reshape(f32[2,128,256]{2,1,0:T(8,128)S(1)} %maximum_subtract_fusion.1) | data formatting | bytes 524288 | tf_op jit(solution)/shard_map/reshape | solution.py:43
  262.1 8.0 reduce_sum.29
  273.4 3.4 psum.51
  276.9 341.1 %all_gather.23 = f32[128,4,2,128]{3,1,2,0:T(4,128)S(1)} all-gather(f32[1,4,2,128]{3,1,2,0:T(4,128)S(1)} %copy.1565), channel_id=1, replica_groups=mesh['tile'=128,'sub'=2] {'tile'}, dimensions={0}, use_global_device_ids=true | all-gather | bytes 528384 | tf_op jit(solution)/shard_map/all_gather | solution.py:54
  621.1 3.0 collective-permute-start.6
  627.1 347.0 %all_gather.24 = f32[128,4,2,128]{3,1,2,0:T(4,128)S(1)} all-gather(f32[1,4,2,128]{3,1,2,0:T(4,128)S(1)} %copy.1573), channel_id=1, replica_groups=mesh['tile'=128,'sub'=2] {'tile'}, dimensions={0}, use_global_device_ids=true | all-gather | bytes 528384 | tf_op jit(solution)/shard_map/all_gather | solution.py:54
  976.6 3.1 psum.53
  984.8 89.8 %all-gather.10.cloned.1.call-done = f32[128,4,2,256]{3,1,2,0:T(4,128)} async-done(((f32[1,4,2,256]{3,1,2,0:T(4,128)}), f32[128,4,2,256]{3,1,2,0:T(4,128)}) %all-gather.10.cloned.1.call-update) | async-done | bytes 1048592 | tf_op jit(solution)/shard_map/all_gather | solution.py:52
  1079.9 3.1 psum.54
  1088.3 96.6 %all-gather.12.cloned.1.call-done = f32[128,4,2,256]{3,1,2,0:T(4,128)} async-done(((f32[1,4,2,256]{3,1,2,0:T(4,128)}), f32[128,4,2,256]{3,1,2,0:T(4,128)}) %all-gather.12.cloned.1.call-update) | async-done | bytes 1048592 | tf_op jit(solution)/shard_map/all_gather | solution.py:52
  1190.6 3.1 psum.55
  1195.0 3.0 collective-permute-start.12
  1199.2 96.3 %all-gather.14.cloned.1.call-done = f32[128,4,2,256]{3,1,2,0:T(4,128)} async-done(((f32[1,4,2,256]{3,1,2,0:T(4,128)}), f32[128,4,2,256]{3,1,2,0:T(4,128)}) %all-gather.14.cloned.1.call-update) | async-done | bytes 1048592 | tf_op jit(solution)/shard_map/all_gather | solution.py:52
  (284 shorter events, 72.2 us)
Async XLA Ops:
  7.2 126.2 %copy-start = (f32[128,256]{1,0:T(8,128)S(1)}, f32[128,256]{1,0:T(8,128)}, u32[]{:S(2)}) copy-start(f32[128,256]{1,0:T(8,128)} %param.6) | copy-start | bytes 393220
  7.2 140.4 %copy-start.1 = (f32[2,128,256]{2,1,0:T(8,128)S(1)}, f32[2,128,256]{2,1,0:T(8,128)}, u32[]{:S(2)}) copy-start(f32[2,128,256]{2,1,0:T(8,128)} %param.7) | copy-start | bytes 786436
  7.2 117.2 %all-gather.6.cloned.1.call-start = ((), (), s32[]{:S(2)}) async-start(), calls=%async_computation | async-start | bytes 1056768 | tf_op jit(solution)/shard_map/all_gather | solution.py:52
  18.6 220.9 %all-gather.8.cloned.1.call-start = ((), (), s32[]{:S(2)}) async-start(), calls=%async_computation.1 | async-start | bytes 1056768 | tf_op jit(solution)/shard_map/all_gather | solution.py:52
  18.7 111.0 %collective-permute-start.1 = (f32[2,1,256]{1,0,2:T(2,128)}, f32[2,1,256]{1,0,2:T(2,128)}, u32[]{:S(2)}, u32[]{:S(2)}) collective-permute-start(f32[2,1,256]{1,0,2:T(2,128)} %get-tuple-element.129), channel_id=1, source_target_pairs={{1,0},{3,2},{5,4},{7,6},{9,8},{11,10},{13,12},{15,14},{17,16},{19,... | collective-permute-start | bytes 6152 | tf_op jit(solution)/shard_map/ppermute | solution.py:20
  20.0 109.3 %collective-permute-start = (f32[2,1,256]{2,0,1:T(2,128)S(1)}, f32[2,1,256]{2,0,1:T(2,128)S(1)}, u32[]{:S(2)}, u32[]{:S(2)}) collective-permute-start(f32[2,1,256]{2,0,1:T(2,128)S(1)} %copy.1640), channel_id=1, source_target_pairs={{0,1},{2,3},{4,5},{6,7},{8,9},{10,11},{12,13},{14,15},{16,17},{18,... | collective-permute-start | bytes 6152 | tf_op jit(solution)/shard_map/ppermute | solution.py:17
  137.7 936.9 %all-gather.10.cloned.1.call-start = ((), (), s32[]{:S(2)}) async-start(), calls=%async_computation.2 | async-start | bytes 1056768 | tf_op jit(solution)/shard_map/all_gather | solution.py:52
  179.9 64.0 %copy-start.2 = (f32[2,128,256]{2,1,0:T(8,128)S(1)}, f32[2,128,256]{2,1,0:T(8,128)}, u32[]{:S(2)}) copy-start(f32[2,128,256]{2,1,0:T(8,128)} %param.5) | copy-start | bytes 786436
  192.5 50.0 %collective-permute-start.2 = (f32[2,1,256]{2,1,0:T(1,128)S(1)}, f32[2,1,256]{2,1,0:T(1,128)S(1)}, u32[]{:S(2)}, u32[]{:S(2)}) collective-permute-start(f32[2,1,256]{2,1,0:T(1,128)S(1)} %get-tuple-element.122), channel_id=1, source_target_pairs={{0,1},{2,3},{4,5},{6,7},{8,9},{10,11},{12,13},{14,15},{16,17},{18,... | collective-permute-start | bytes 6152 | tf_op jit(solution)/shard_map/ppermute | solution.py:17
  194.6 47.9 %collective-permute-start.3 = (f32[2,1,256]{2,1,0:T(1,128)S(1)}, f32[2,1,256]{2,1,0:T(1,128)S(1)}, u32[]{:S(2)}, u32[]{:S(2)}) collective-permute-start(f32[2,1,256]{2,1,0:T(1,128)S(1)} %get-tuple-element.119), channel_id=1, source_target_pairs={{1,0},{3,2},{5,4},{7,6},{9,8},{11,10},{13,12},{15,14},{17,16},{19,... | collective-permute-start | bytes 6152 | tf_op jit(solution)/shard_map/ppermute | solution.py:20
  244.0 375.6 %copy-start.4 = (f32[64,128]{1,0:T(8,128)S(1)}, f32[64,128]{1,0:T(8,128)}, u32[]{:S(2)}) copy-start(f32[64,128]{1,0:T(8,128)} %get-tuple-element.156) | copy-start | bytes 98308
  270.3 349.0 %collective-permute-start.4 = (f32[2,1,128]{2,0,1:T(2,128)S(1)}, f32[2,1,128]{2,0,1:T(2,128)S(1)}, u32[]{:S(2)}, u32[]{:S(2)}) collective-permute-start(f32[2,1,128]{2,0,1:T(2,128)S(1)} %bitcast.453), channel_id=1, source_target_pairs={{0,1},{2,3},{4,5},{6,7},{8,9},{10,11},{12,13},{14,15},{16,17},{18,... | collective-permute-start | bytes 3080 | tf_op jit(solution)/shard_map/ppermute | solution.py:17
  271.7 347.7 %collective-permute-start.5 = (f32[2,1,128]{2,0,1:T(2,128)S(1)}, f32[2,1,128]{2,0,1:T(2,128)S(1)}, u32[]{:S(2)}, u32[]{:S(2)}) collective-permute-start(f32[2,1,128]{2,0,1:T(2,128)S(1)} %bitcast.449), channel_id=1, source_target_pairs={{1,0},{3,2},{5,4},{7,6},{9,8},{11,10},{13,12},{15,14},{17,16},{19,... | collective-permute-start | bytes 3080 | tf_op jit(solution)/shard_map/ppermute | solution.py:20
  619.8 355.7 %collective-permute-start.7 = (f32[2,1,128]{2,0,1:T(2,128)S(1)}, f32[2,1,128]{2,0,1:T(2,128)S(1)}, u32[]{:S(2)}, u32[]{:S(2)}) collective-permute-start(f32[2,1,128]{2,0,1:T(2,128)S(1)} %bitcast.451), channel_id=1, source_target_pairs={{1,0},{3,2},{5,4},{7,6},{9,8},{11,10},{13,12},{15,14},{17,16},{19,... | collective-permute-start | bytes 3080 | tf_op jit(solution)/shard_map/ppermute | solution.py:20
  621.1 354.4 %collective-permute-start.6 = (f32[2,1,128]{2,0,1:T(2,128)S(1)}, f32[2,1,128]{2,0,1:T(2,128)S(1)}, u32[]{:S(2)}, u32[]{:S(2)}) collective-permute-start(f32[2,1,128]{2,0,1:T(2,128)S(1)} %bitcast.447), channel_id=1, source_target_pairs={{0,1},{2,3},{4,5},{6,7},{8,9},{10,11},{12,13},{14,15},{16,17},{18,... | collective-permute-start | bytes 3080 | tf_op jit(solution)/shard_map/ppermute | solution.py:17
  979.7 205.2 %all-gather.12.cloned.1.call-start = ((), (), s32[]{:S(2)}) async-start(), calls=%async_computation.3 | async-start | bytes 1056768 | tf_op jit(solution)/shard_map/all_gather | solution.py:52
  979.8 97.7 %collective-permute-start.8 = (f32[2,1,256]{2,1,0:T(1,128)S(1)}, f32[2,1,256]{2,1,0:T(1,128)S(1)}, u32[]{:S(2)}, u32[]{:S(2)}) collective-permute-start(f32[2,1,256]{2,1,0:T(1,128)S(1)} %get-tuple-element.108), channel_id=1, source_target_pairs={{0,1},{2,3},{4,5},{6,7},{8,9},{10,11},{12,13},{14,15},{16,17},{18,... | collective-permute-start | bytes 6152 | tf_op jit(solution)/shard_map/ppermute | solution.py:17
  981.9 95.7 %collective-permute-start.9 = (f32[2,1,256]{2,1,0:T(1,128)S(1)}, f32[2,1,256]{2,1,0:T(1,128)S(1)}, u32[]{:S(2)}, u32[]{:S(2)}) collective-permute-start(f32[2,1,256]{2,1,0:T(1,128)S(1)} %get-tuple-element.105), channel_id=1, source_target_pairs={{1,0},{3,2},{5,4},{7,6},{9,8},{11,10},{13,12},{15,14},{17,16},{19,... | collective-permute-start | bytes 6152 | tf_op jit(solution)/shard_map/ppermute | solution.py:20
  1083.0 212.5 %all-gather.14.cloned.1.call-start = ((), (), s32[]{:S(2)}) async-start(), calls=%async_computation.4 | async-start | bytes 1056768 | tf_op jit(solution)/shard_map/all_gather | solution.py:52
  1083.1 104.7 %collective-permute-start.10 = (f32[2,1,256]{2,1,0:T(1,128)S(1)}, f32[2,1,256]{2,1,0:T(1,128)S(1)}, u32[]{:S(2)}, u32[]{:S(2)}) collective-permute-start(f32[2,1,256]{2,1,0:T(1,128)S(1)} %get-tuple-element.94), channel_id=1, source_target_pairs={{0,1},{2,3},{4,5},{6,7},{8,9},{10,11},{12,13},{14,15},{16,17},{18,... | collective-permute-start | bytes 6152 | tf_op jit(solution)/shard_map/ppermute | solution.py:17
  1085.1 102.6 %collective-permute-start.11 = (f32[2,1,256]{2,1,0:T(1,128)S(1)}, f32[2,1,256]{2,1,0:T(1,128)S(1)}, u32[]{:S(2)}, u32[]{:S(2)}) collective-permute-start(f32[2,1,256]{2,1,0:T(1,128)S(1)} %get-tuple-element.91), channel_id=1, source_target_pairs={{1,0},{3,2},{5,4},{7,6},{9,8},{11,10},{13,12},{15,14},{17,16},{19,... | collective-permute-start | bytes 6152 | tf_op jit(solution)/shard_map/ppermute | solution.py:20
  1189.8 111.5 %copy-start.3 = (f32[2,128,256]{2,1,0:T(8,128)}, f32[2,128,256]{2,1,0:T(8,128)S(1)}, u32[]{:S(2)}) copy-start(f32[2,128,256]{2,1,0:T(8,128)S(1)} %fusion.13) | copy-start | bytes 786436
  1193.7 104.5 %collective-permute-start.13 = (f32[2,1,256]{2,1,0:T(1,128)S(1)}, f32[2,1,256]{2,1,0:T(1,128)S(1)}, u32[]{:S(2)}, u32[]{:S(2)}) collective-permute-start(f32[2,1,256]{2,1,0:T(1,128)S(1)} %get-tuple-element.77), channel_id=1, source_target_pairs={{1,0},{3,2},{5,4},{7,6},{9,8},{11,10},{13,12},{15,14},{17,16},{19,... | collective-permute-start | bytes 6152 | tf_op jit(solution)/shard_map/ppermute | solution.py:20
  1195.0 103.5 %collective-permute-start.12 = (f32[2,1,256]{2,0,1:T(2,128)S(1)}, f32[2,1,256]{2,0,1:T(2,128)S(1)}, u32[]{:S(2)}, u32[]{:S(2)}) collective-permute-start(f32[2,1,256]{2,0,1:T(2,128)S(1)} %get-tuple-element.80), channel_id=1, source_target_pairs={{0,1},{2,3},{4,5},{6,7},{8,9},{10,11},{12,13},{14,15},{16,17},{18,... | collective-permute-start | bytes 6152 | tf_op jit(solution)/shard_map/ppermute | solution.py:17
  (1 other events, 26.2 us)
Sparse Core Ops, SparseCore 0:
  18.8 105.5 all-gather.5
  137.9 101.6 all-gather.7
  979.8 94.7 all-gather.9
  1083.1 101.6 all-gather.11
  1193.8 101.6 all-gather.13
where the time goes:
time: 1310 us
  blocking collectives  710 us (54%)
  waiting for transfers between devices  421 us (32%)
  local copies, waits for them, and re-layouts  94.2 us (7%)
  other arithmetic  41.1 us (3%)
  starting transfers between devices  26.9 us (2%)
  between operations  15.2 us (1%)
    all_gather x2, blocking collectives, across_sides(): everyone = lax.all_gather(side_rows[None], 'tile', axis=0, tiled=True)  688 us
    all_gather x5, waiting for transfers between devices, across_sides(): everyone = lax.all_gather(side_rows[None], 'tile', axis=0, tiled=True)  421 us
    another operation x2, local copies, waits for them, and re-layouts, body(): noise_terms = jnp.stack([noise_diag[0], noise_diag[1], cross_noise])  27.8 us
    reshape x2, local copies, waits for them, and re-layouts, coarsen_sum(): return values.reshape(new_shape).sum(axis=(-3, -1))  27.8 us
  transfers between devices with their start and end apart: 19, of which 5 were waited for; matrix products, arithmetic and copies ran while one was open for 7% of the time, Pallas kernels for 0%

commit v1 on v0

--- a/solution.py
+++ b/solution.py
@@ -49,7 +49,10 @@
 
 def across_sides(side_rows, link_cols, grid_level):
     if grid_level == "fine":
-        everyone = lax.all_gather(side_rows[None], "tile", axis=0, tiled=True)
+        everyone = jnp.concatenate(
+            lax.all_to_all(jnp.stack([side_rows[None]] * lax.axis_size("tile")), "tile", 0, 0),
+            axis=0,
+        )
     else:
         everyone = lax.all_gather(side_rows[None], "tile", axis=0, tiled=True)
     across = everyone[link_cols[0], link_cols[1]]

time: 1310 us -> 1010 us (0.77)
  waiting for transfers between devices: 421 us -> 87.9 us
  starting transfers between devices: 26.9 us -> 79.5 us
  between operations: 15.2 us -> 1.82 us
    all_gather x5 -> x0, waiting for transfers between devices: 421 us -> none  [across_sides(): everyone = lax.all_gather(side_rows[None], 'tile', axis=0, tiled=True)]
    all_to_all x0 -> x5, waiting for transfers between devices: none -> 87.9 us  [across_sides(): lax.all_to_all(jnp.stack([side_rows[None]] * lax.axis_size('tile')), 'til...]
    all_to_all x0 -> x5, starting transfers between devices: none -> 44.6 us  [across_sides(): lax.all_to_all(jnp.stack([side_rows[None]] * lax.axis_size('tile')), 'til...]
  transfers between devices with their start and end apart: 19 -> 19, of which waited for: 5 -> 4; matrix products, arithmetic and copies ran while one was open for 7% -> 8% of each run, Pallas kernels for 0% -> 0%
where the time goes in v1:
time: 1010 us
  blocking collectives  708 us (70%)
  waiting for transfers between devices  87.9 us (9%)
  local copies, waits for them, and re-layouts  87.2 us (9%)
  starting transfers between devices  79.5 us (8%)
  other arithmetic  48.4 us (5%)
    all_gather x2, blocking collectives, across_sides(): everyone = lax.all_gather(side_rows[None], 'tile', axis=0, tiled=True)  689 us
    all_to_all x5, waiting for transfers between devices, across_sides(): lax.all_to_all(jnp.stack([side_rows[None]] * lax.axis_size('tile')), 'til...  87.9 us
    all_to_all x5, starting transfers between devices, across_sides(): lax.all_to_all(jnp.stack([side_rows[None]] * lax.axis_size('tile')), 'til...  44.6 us
    another operation x2, local copies, waits for them, and re-layouts, body(): noise_terms = jnp.stack([noise_diag[0], noise_diag[1], cross_noise])  27.8 us
    reshape x2, local copies, waits for them, and re-layouts, coarsen_sum(): return values.reshape(new_shape).sum(axis=(-3, -1))  27.8 us
    ppermute x7, starting transfers between devices, with_halo(): lax.ppermute(lax.slice_in_dim(block, block.shape[dim] - width, None, axis...  25.9 us
    reduce_sum x3, other arithmetic, coarsen_sum(): return values.reshape(new_shape).sum(axis=(-3, -1))  24.6 us
  transfers between devices with their start and end apart: 19, of which 4 were waited for; matrix products, arithmetic and copies ran while one was open for 8% of the time, Pallas kernels for 0%

profile of v1, /device:TPU:2, one launch (start us, length us, event | category | flops | bytes accessed | tf_op | source)
XLA Modules:
  0.0 1012.6 jit_solution(10241292172351659967)
XLA Ops:
  11.0 15.6 %all-to-all-start = ((f32[128,1,4,2,256]{4,3,2,1,0:T(2,128)}), f32[128,1,4,2,256]{4,3,2,1,0:T(2,128)S(1)}, u32[]{:S(2)}, u32[]{:S(2)}) async-start(f32[128,1,4,2,256]{4,3,2,1,0:T(2,128)} %stack.213), calls=%async_computation | async-start | bytes 2097152 | tf_op jit(solution)/shard_map/all_to_all | solution.py:53
  27.8 4.4 collective-permute-start
  35.8 20.4 %all-to-all-done = f32[128,1,4,2,256]{4,3,2,1,0:T(2,128)S(1)} async-done(((f32[128,1,4,2,256]{4,3,2,1,0:T(2,128)}), f32[128,1,4,2,256]{4,3,2,1,0:T(2,128)S(1)}, u32[]{:S(2)}, u32[]{:S(2)}) %all-to-all-start) | async-done | bytes 1048608 | tf_op jit(solution)/shard_map/all_to_all | solution.py:53
  65.7 7.8 all-to-all-start.1
  73.7 18.1 %stack.220 = f32[2,64,2,128,2]{4,3,2,1,0:T(8,128)} reshape(f32[2,128,256]{2,1,0:T(8,128)S(1)} %copy-done.1) | data formatting | bytes 524288 | tf_op jit(solution)/shard_map/stack | solution.py:137
  91.8 9.7 reshape.589
  101.5 9.7 stack.221
  111.2 4.6 reduce_sum.27
  115.8 12.0 %maximum_reduce_fusion = f32[3,64,128]{2,1,0:T(8,128)S(1)} fusion(f32[1,64,2,128,2]{4,3,2,1,0:T(8,128)} %stack.221, f32[2,64,2,128,2]{4,3,2,1,0:T(8,128)} %stack.220), kind=kLoop, calls=%fused_computation.7 | loop fusion | flops 172032 | bytes 491520 | tf_op jit(solution)/shard_map/reduce_sum | solution.py:43
  129.1 4.4 collective-permute-start.2
  139.9 18.1 %reshape.591 = f32[2,64,2,128,2]{4,3,2,1,0:T(8,128)} reshape(f32[2,128,256]{2,1,0:T(8,128)S(1)} %copy.1203) | data formatting | bytes 524288 | tf_op jit(solution)/shard_map/reshape | solution.py:43
  158.0 8.0 reduce_sum.29
  169.3 3.4 psum.51
  172.8 342.3 %all_gather.6 = f32[128,4,2,128]{3,1,2,0:T(4,128)S(1)} all-gather(f32[1,4,2,128]{3,1,2,0:T(4,128)S(1)} %copy.1206), channel_id=1, replica_groups=mesh['tile'=128,'sub'=2] {'tile'}, dimensions={0}, use_global_device_ids=true | all-gather | bytes 528384 | tf_op jit(solution)/shard_map/all_gather | solution.py:57
  524.1 347.0 %all_gather.7 = f32[128,4,2,128]{3,1,2,0:T(4,128)S(1)} all-gather(f32[1,4,2,128]{3,1,2,0:T(4,128)S(1)} %copy.1214), channel_id=1, replica_groups=mesh['tile'=128,'sub'=2] {'tile'}, dimensions={0}, use_global_device_ids=true | all-gather | bytes 528384 | tf_op jit(solution)/shard_map/all_gather | solution.py:57
  877.8 5.3 all-to-all-start.2
  884.4 4.5 collective-permute-start.8
  890.5 22.7 %all-to-all-done.2 = f32[128,1,4,2,256]{4,3,2,1,0:T(2,128)S(1)} async-done(((f32[128,1,4,2,256]{4,3,2,1,0:T(2,128)}), f32[128,1,4,2,256]{4,3,2,1,0:T(2,128)S(1)}, u32[]{:S(2)}, u32[]{:S(2)}) %all-to-all-start.2) | async-done | bytes 1048608 | tf_op jit(solution)/shard_map/all_to_all | solution.py:53
  922.6 7.8 all-to-all-start.3
  931.6 4.5 collective-permute-start.10
  937.7 22.3 %all-to-all-done.3 = f32[128,1,4,2,256]{4,3,2,1,0:T(2,128)S(1)} async-done(((f32[128,1,4,2,256]{4,3,2,1,0:T(2,128)}), f32[128,1,4,2,256]{4,3,2,1,0:T(2,128)S(1)}, u32[]{:S(2)}, u32[]{:S(2)}) %all-to-all-start.3) | async-done | bytes 1048608 | tf_op jit(solution)/shard_map/all_to_all | solution.py:53
  969.4 8.1 all-to-all-start.4
  978.8 3.7 collective-permute-start.12
  984.7 22.5 %all-to-all-done.4 = f32[128,1,4,2,256]{4,3,2,1,0:T(2,128)S(1)} async-done(((f32[128,1,4,2,256]{4,3,2,1,0:T(2,128)}), f32[128,1,4,2,256]{4,3,2,1,0:T(2,128)S(1)}, u32[]{:S(2)}, u32[]{:S(2)}) %all-to-all-start.4) | async-done | bytes 1048608 | tf_op jit(solution)/shard_map/all_to_all | solution.py:53
  (243 shorter events, 83.9 us)
Async XLA Ops:
  0.6 73.1 %copy-start.1 = (f32[2,128,256]{2,1,0:T(8,128)S(1)}, f32[2,128,256]{2,1,0:T(8,128)}, u32[]{:S(2)}) copy-start(f32[2,128,256]{2,1,0:T(8,128)} %param.7) | copy-start | bytes 786436
  11.0 80.8 %copy-start = (f32[128,256]{1,0:T(8,128)S(1)}, f32[128,256]{1,0:T(8,128)}, u32[]{:S(2)}) copy-start(f32[128,256]{1,0:T(8,128)} %param.6) | copy-start | bytes 393220
  11.0 45.2 %all-to-all-start = ((f32[128,1,4,2,256]{4,3,2,1,0:T(2,128)}), f32[128,1,4,2,256]{4,3,2,1,0:T(2,128)S(1)}, u32[]{:S(2)}, u32[]{:S(2)}) async-start(f32[128,1,4,2,256]{4,3,2,1,0:T(2,128)} %stack.213), calls=%async_computation | async-start | bytes 2097152 | tf_op jit(solution)/shard_map/all_to_all | solution.py:53
  26.5 30.9 %collective-permute-start.1 = (f32[2,1,256]{1,2,0:T(8,128)}, f32[2,1,256]{1,2,0:T(8,128)}, u32[]{:S(2)}, u32[]{:S(2)}) collective-permute-start(f32[2,1,256]{1,2,0:T(8,128)} %get-tuple-element.118), channel_id=1, source_target_pairs={{1,0},{3,2},{5,4},{7,6},{9,8},{11,10},{13,12},{15,14},{17,16},{19,... | collective-permute-start | bytes 6152 | tf_op jit(solution)/shard_map/ppermute | solution.py:20
  27.8 30.6 %collective-permute-start = (f32[2,1,256]{1,2,0:T(8,128)}, f32[2,1,256]{1,2,0:T(8,128)}, u32[]{:S(2)}, u32[]{:S(2)}) collective-permute-start(f32[2,1,256]{1,2,0:T(8,128)} %get-tuple-element.119), channel_id=1, source_target_pairs={{0,1},{2,3},{4,5},{6,7},{8,9},{10,11},{12,13},{14,15},{16,17},{18,... | collective-permute-start | bytes 6152 | tf_op jit(solution)/shard_map/ppermute | solution.py:17
  65.7 69.4 %all-to-all-start.1 = ((f32[128,1,4,2,256]{4,3,2,1,0:T(2,128)}), f32[128,1,4,2,256]{4,3,2,1,0:T(2,128)S(1)}, u32[]{:S(2)}, u32[]{:S(2)}) async-start(f32[128,1,4,2,256]{4,3,2,1,0:T(2,128)} %stack.226), calls=%async_computation.1 | async-start | bytes 2097152 | tf_op jit(solution)/shard_map/all_to_all | solution.py:53
  111.2 16.6 %copy-start.2 = (f32[2,1,256]{1,2,0:T(8,128)S(1)}, f32[2,1,256]{1,2,0:T(8,128)}, u32[]{:S(2)}) copy-start(f32[2,1,256]{1,2,0:T(8,128)} %get-tuple-element.108) | copy-start | bytes 6148
  127.8 8.6 collective-permute-start.3
  129.1 8.2 collective-permute-start.2
  166.2 350.2 %collective-permute-start.4 = (f32[2,1,128]{2,0,1:T(2,128)S(1)}, f32[2,1,128]{2,0,1:T(2,128)S(1)}, u32[]{:S(2)}, u32[]{:S(2)}) collective-permute-start(f32[2,1,128]{2,0,1:T(2,128)S(1)} %bitcast.499), channel_id=1, source_target_pairs={{0,1},{2,3},{4,5},{6,7},{8,9},{10,11},{12,13},{14,15},{16,17},{18,... | collective-permute-start | bytes 3080 | tf_op jit(solution)/shard_map/ppermute | solution.py:17
  167.6 348.9 %collective-permute-start.5 = (f32[2,1,128]{2,0,1:T(2,128)S(1)}, f32[2,1,128]{2,0,1:T(2,128)S(1)}, u32[]{:S(2)}, u32[]{:S(2)}) collective-permute-start(f32[2,1,128]{2,0,1:T(2,128)S(1)} %bitcast.495), channel_id=1, source_target_pairs={{1,0},{3,2},{5,4},{7,6},{9,8},{11,10},{13,12},{15,14},{17,16},{19,... | collective-permute-start | bytes 3080 | tf_op jit(solution)/shard_map/ppermute | solution.py:20
  516.9 355.7 %collective-permute-start.7 = (f32[2,1,128]{2,0,1:T(2,128)S(1)}, f32[2,1,128]{2,0,1:T(2,128)S(1)}, u32[]{:S(2)}, u32[]{:S(2)}) collective-permute-start(f32[2,1,128]{2,0,1:T(2,128)S(1)} %bitcast.497), channel_id=1, source_target_pairs={{1,0},{3,2},{5,4},{7,6},{9,8},{11,10},{13,12},{15,14},{17,16},{19,... | collective-permute-start | bytes 3080 | tf_op jit(solution)/shard_map/ppermute | solution.py:20
  518.2 354.4 %collective-permute-start.6 = (f32[2,1,128]{2,0,1:T(2,128)S(1)}, f32[2,1,128]{2,0,1:T(2,128)S(1)}, u32[]{:S(2)}, u32[]{:S(2)}) collective-permute-start(f32[2,1,128]{2,0,1:T(2,128)S(1)} %bitcast.493), channel_id=1, source_target_pairs={{0,1},{2,3},{4,5},{6,7},{8,9},{10,11},{12,13},{14,15},{16,17},{18,... | collective-permute-start | bytes 3080 | tf_op jit(solution)/shard_map/ppermute | solution.py:17
  877.8 35.3 %all-to-all-start.2 = ((f32[128,1,4,2,256]{4,3,2,1,0:T(2,128)}), f32[128,1,4,2,256]{4,3,2,1,0:T(2,128)S(1)}, u32[]{:S(2)}, u32[]{:S(2)}) async-start(f32[128,1,4,2,256]{4,3,2,1,0:T(2,128)} %stack.244), calls=%async_computation.2 | async-start | bytes 2097152 | tf_op jit(solution)/shard_map/all_to_all | solution.py:53
  883.1 31.2 %collective-permute-start.9 = (f32[2,1,256]{1,2,0:T(8,128)S(1)}, f32[2,1,256]{1,2,0:T(8,128)}, u32[]{:S(2)}, u32[]{:S(2)}) collective-permute-start(f32[2,1,256]{1,2,0:T(8,128)S(1)} %get-tuple-element.96), channel_id=1, source_target_pairs={{1,0},{3,2},{5,4},{7,6},{9,8},{11,10},{13,12},{15,14},{17,16},{19,... | collective-permute-start | bytes 6152 | tf_op jit(solution)/shard_map/ppermute | solution.py:20
  884.4 30.9 %collective-permute-start.8 = (f32[2,1,256]{1,2,0:T(8,128)}, f32[2,1,256]{1,2,0:T(8,128)}, u32[]{:S(2)}, u32[]{:S(2)}) collective-permute-start(f32[2,1,256]{1,2,0:T(8,128)} %get-tuple-element.97), channel_id=1, source_target_pairs={{0,1},{2,3},{4,5},{6,7},{8,9},{10,11},{12,13},{14,15},{16,17},{18,... | collective-permute-start | bytes 6152 | tf_op jit(solution)/shard_map/ppermute | solution.py:17
  922.6 37.4 %all-to-all-start.3 = ((f32[128,1,4,2,256]{4,3,2,1,0:T(2,128)}), f32[128,1,4,2,256]{4,3,2,1,0:T(2,128)S(1)}, u32[]{:S(2)}, u32[]{:S(2)}) async-start(f32[128,1,4,2,256]{4,3,2,1,0:T(2,128)} %stack.254), calls=%async_computation.3 | async-start | bytes 2097152 | tf_op jit(solution)/shard_map/all_to_all | solution.py:53
  930.3 30.9 %collective-permute-start.11 = (f32[2,1,256]{1,2,0:T(8,128)S(1)}, f32[2,1,256]{1,2,0:T(8,128)}, u32[]{:S(2)}, u32[]{:S(2)}) collective-permute-start(f32[2,1,256]{1,2,0:T(8,128)S(1)} %get-tuple-element.88), channel_id=1, source_target_pairs={{1,0},{3,2},{5,4},{7,6},{9,8},{11,10},{13,12},{15,14},{17,16},{19,... | collective-permute-start | bytes 6152 | tf_op jit(solution)/shard_map/ppermute | solution.py:20
  931.6 30.6 %collective-permute-start.10 = (f32[2,1,256]{1,2,0:T(8,128)}, f32[2,1,256]{1,2,0:T(8,128)}, u32[]{:S(2)}, u32[]{:S(2)}) collective-permute-start(f32[2,1,256]{1,2,0:T(8,128)} %get-tuple-element.89), channel_id=1, source_target_pairs={{0,1},{2,3},{4,5},{6,7},{8,9},{10,11},{12,13},{14,15},{16,17},{18,... | collective-permute-start | bytes 6152 | tf_op jit(solution)/shard_map/ppermute | solution.py:17
  969.4 37.8 %all-to-all-start.4 = ((f32[128,1,4,2,256]{4,3,2,1,0:T(2,128)}), f32[128,1,4,2,256]{4,3,2,1,0:T(2,128)S(1)}, u32[]{:S(2)}, u32[]{:S(2)}) async-start(f32[128,1,4,2,256]{4,3,2,1,0:T(2,128)} %stack.264), calls=%async_computation.4 | async-start | bytes 2097152 | tf_op jit(solution)/shard_map/all_to_all | solution.py:53
  977.5 31.0 %collective-permute-start.13 = (f32[2,1,256]{1,0,2:T(2,128)S(1)}, f32[2,1,256]{1,0,2:T(2,128)}, u32[]{:S(2)}, u32[]{:S(2)}) collective-permute-start(f32[2,1,256]{1,0,2:T(2,128)S(1)} %get-tuple-element.82), channel_id=1, source_target_pairs={{1,0},{3,2},{5,4},{7,6},{9,8},{11,10},{13,12},{15,14},{17,16},{19,... | collective-permute-start | bytes 6152 | tf_op jit(solution)/shard_map/ppermute | solution.py:20
  978.8 29.2 %collective-permute-start.12 = (f32[2,1,256]{2,0,1:T(2,128)S(1)}, f32[2,1,256]{2,0,1:T(2,128)S(1)}, u32[]{:S(2)}, u32[]{:S(2)}) collective-permute-start(f32[2,1,256]{2,0,1:T(2,128)S(1)} %copy.1267), channel_id=1, source_target_pairs={{0,1},{2,3},{4,5},{6,7},{8,9},{10,11},{12,13},{14,15},{16,17},{18,... | collective-permute-start | bytes 6152 | tf_op jit(solution)/shard_map/ppermute | solution.py:17
